TPU v7x, 32 devices: a whole 2x2x4 slice. The times are simulated.
32 devices in a mesh: dp: 16 (over z, x, core), tensor: 2 (over y).
Axes of the slice: x: 2, y: 2, z: 4, core: 2. Of those that a mesh axis runs over, the one named last changes fastest.
Arguments:
- stream: bfloat16 [16, 1536, 1024], P('dp')
- validity: int32 [16], P('dp'), may hold values from 0 to 1, as said below
- norm1_gain: float32 [1024], replicated, may hold values from 0.5 to 1.5
- norm1_bias: float32 [1024], replicated, may hold values from -1.75 to 1.75
- qkv_weight: bfloat16 [1024, 3, 1024], P(None, None, 'tensor'), may hold values from -0.25 to 0.25
- qkv_bias: float32 [2, 1024], P(None, 'tensor'), may hold values from -1.75 to 1.75
- proj_weight: bfloat16 [1024, 1024], P('tensor'), may hold values from -1 to 1
- proj_bias: float32 [1024], replicated, may hold values from -1.75 to 1.75
- layer_scale1: float32 [1024], replicated, may hold values from 0.25 to 1.75
- norm2_gain: float32 [1024], replicated, may hold values from 0.5 to 1.5
- norm2_bias: float32 [1024], replicated, may hold values from -1.75 to 1.75
- fc1_weight: bfloat16 [1024, 4096], P(None, 'tensor'), may hold values from -0.1875 to 0.1875
- fc1_bias: float32 [4096], P('tensor'), may hold values from -3 to 3
- fc2_weight: bfloat16 [4096, 1024], P('tensor'), may hold values from -0.09375 to 0.09375
- fc2_bias: float32 [1024], replicated, may hold values from -1.75 to 1.75
- layer_scale2: float32 [1024], replicated, may hold values from 0.25 to 1.75
- cotangent: bfloat16 [16, 1536, 1024], P('dp'), may hold values from -6 to 6
Outputs:
- block_output: bfloat16 [16, 1536, 1024], P('dp')
- stream_grad: bfloat16 [16, 1536, 1024], P('dp')
- norm1_gain_grad: float32 [1024], replicated
- norm1_bias_grad: float32 [1024], replicated
- qkv_weight_grad: float32 [1024, 3, 1024], P(None, None, 'tensor')
- qkv_bias_grad: float32 [2, 1024], P(None, 'tensor')
- proj_weight_grad: float32 [1024, 1024], P('tensor')
- proj_bias_grad: float32 [1024], replicated
- layer_scale1_grad: float32 [1024], replicated
- norm2_gain_grad: float32 [1024], replicated
- norm2_bias_grad: float32 [1024], replicated
- fc1_weight_grad: float32 [1024, 4096], P(None, 'tensor')
- fc1_bias_grad: float32 [4096], P('tensor')
- fc2_weight_grad: float32 [4096, 1024], P('tensor')
- fc2_bias_grad: float32 [1024], replicated
- layer_scale2_grad: float32 [1024], replicated
- root_means: float32 [5], replicated
Inputs may be any that keep to these rules, and one draw needn't show every extreme that they name: `validity`: each slot's flag is 1 for an image and 0 for padding; at least one slot holds an image; positions 1370 and above of every slot are padding.
All inputs are finite; a program needn't handle non-finite values.
Results may differ from a plain program's by a relative error of at most 0.02.
Values may be sent and summed in bfloat16 or wider, within the bound.
No kernel may reach another device: no remote copies, remote signals or barrier semaphores. Data moves between devices by JAX's collectives and lax.ppermute only.
A program may use at most 320 MiB of HBM per device.

v0:
```python
import jax
import jax.numpy as jnp
from jax import lax
from jax.sharding import PartitionSpec as P

HEAD_DIM = 64
SEQ = 1370
PAD_UNIT = 512


eps = 1e-06


def normalize(values, gain, shift):
    mean = jnp.mean(values, axis=-1, keepdims=True)
    centered = values - mean
    variance = jnp.mean(centered * centered, axis=-1, keepdims=True)
    inverse = lax.rsqrt(variance + eps)
    normed = centered * inverse
    return (normed * gain + shift, normed, inverse)


def normalize_back(grad_out, normed, inverse, gain):
    scaled = grad_out * gain
    centered = scaled - jnp.mean(scaled, axis=-1, keepdims=True)
    return inverse * (centered - normed * jnp.mean(scaled * normed, axis=-1, keepdims=True))


def attend_forward(query, keyed, valued):
    slots, length, width = query.shape
    heads = width // HEAD_DIM
    queries = query.reshape(slots, length, heads, HEAD_DIM)
    keys = keyed.reshape(slots, length, heads, HEAD_DIM)
    values = valued.reshape(slots, length, heads, HEAD_DIM)
    live = (jnp.arange(length) < SEQ)[None, None, None, :]

    def one_block(index):
        block = lax.dynamic_slice_in_dim(queries, index * PAD_UNIT, PAD_UNIT, 1)
        scores = jnp.einsum(
            "sqhd,skhd->shqk", block, keys, preferred_element_type=jnp.float32
        ) * HEAD_DIM ** (-0.5)
        scores = jnp.where(live, scores, -1e30)
        top = jnp.max(scores, axis=-1, keepdims=True)
        total = jnp.sum(jnp.exp(scores - top), axis=-1, keepdims=True)
        logsum = top + jnp.log(total)
        probs = jnp.exp(scores - logsum).astype(jnp.bfloat16)
        mixed = jnp.einsum("shqk,skhd->sqhd", probs, values, preferred_element_type=jnp.float32)
        return (mixed.astype(jnp.bfloat16), logsum[..., 0])

    mixed, logsums = lax.map(one_block, jnp.arange(length // PAD_UNIT))
    mixed = mixed.transpose(1, 0, 2, 3, 4).reshape(slots, length, width)
    return (mixed, logsums)


def attend_backward(query, keyed, valued, logsums, grad_mixed):
    slots, length, width = query.shape
    heads = width // HEAD_DIM
    queries = query.reshape(slots, length, heads, HEAD_DIM)
    keys = keyed.reshape(slots, length, heads, HEAD_DIM)
    values = valued.reshape(slots, length, heads, HEAD_DIM)
    grads = grad_mixed.reshape(slots, length, heads, HEAD_DIM)
    live = (jnp.arange(length) < SEQ)[None, None, None, :]
    factor = HEAD_DIM ** (-0.5)

    def one_block(carry, index):
        key_acc, value_acc = carry
        block = lax.dynamic_slice_in_dim(queries, index * PAD_UNIT, PAD_UNIT, 1)
        grad_block = lax.dynamic_slice_in_dim(grads, index * PAD_UNIT, PAD_UNIT, 1)
        scores = (
            jnp.einsum("sqhd,skhd->shqk", block, keys, preferred_element_type=jnp.float32) * factor
        )
        scores = jnp.where(live, scores, -1e30)
        probs = jnp.exp(scores - logsums[index][..., None])
        dprob = jnp.einsum(
            "sqhd,skhd->shqk", grad_block, values, preferred_element_type=jnp.float32
        )
        dscore = probs * (dprob - jnp.sum(probs * dprob, axis=-1, keepdims=True))
        dscore_low = dscore.astype(jnp.bfloat16)
        dquery = (
            jnp.einsum("shqk,skhd->sqhd", dscore_low, keys, preferred_element_type=jnp.float32)
            * factor
        )
        key_acc = (
            key_acc
            + jnp.einsum("shqk,sqhd->skhd", dscore_low, block, preferred_element_type=jnp.float32)
            * factor
        )
        value_acc = value_acc + jnp.einsum(
            "shqk,sqhd->skhd",
            probs.astype(jnp.bfloat16),
            grad_block,
            preferred_element_type=jnp.float32,
        )
        return ((key_acc, value_acc), dquery)

    empty = jnp.zeros((slots, length, heads, HEAD_DIM), jnp.float32)
    (grad_key, grad_value), grad_query = lax.scan(
        one_block, (empty, empty), jnp.arange(length // PAD_UNIT)
    )
    grad_query = grad_query.transpose(1, 0, 2, 3, 4).reshape(slots * length, width)
    return (
        grad_query,
        grad_key.reshape(slots * length, width),
        grad_value.reshape(slots * length, width),
    )


def shards(
    stream,
    validity,
    norm1_gain,
    norm1_bias,
    qkv_weight,
    qkv_bias,
    proj_weight,
    proj_bias,
    layer_scale1,
    norm2_gain,
    norm2_bias,
    fc1_weight,
    fc1_bias,
    fc2_weight,
    fc2_bias,
    layer_scale2,
    cotangent,
):
    slots, length, width = stream.shape
    rows = slots * length
    local = qkv_weight.shape[2]
    flat = stream.reshape(rows, width).astype(jnp.float32)
    live = (
        ((validity[:, None] == 1) & (jnp.arange(length)[None, :] < SEQ))
        .astype(jnp.float32)
        .reshape(rows, 1)
    )
    first, normed1, inverse1 = normalize(flat, norm1_gain, norm1_bias)
    first_low = first.astype(jnp.bfloat16)
    projected = jnp.einsum("rd,dcn->rcn", first_low, qkv_weight, preferred_element_type=jnp.float32)
    query = (projected[:, 0] + qkv_bias[0]).astype(jnp.bfloat16).reshape(slots, length, local)
    keyed = projected[:, 1].astype(jnp.bfloat16).reshape(slots, length, local)
    valued = (projected[:, 2] + qkv_bias[1]).astype(jnp.bfloat16).reshape(slots, length, local)
    mixed, logsums = attend_forward(query, keyed, valued)
    mixed_rows = mixed.reshape(rows, local)
    attend_share = jnp.dot(mixed_rows, proj_weight, preferred_element_type=jnp.float32)
    attended = lax.psum(attend_share.astype(jnp.bfloat16), "tensor").astype(jnp.float32) + proj_bias
    after = flat + layer_scale1 * attended
    second, normed2, inverse2 = normalize(after, norm2_gain, norm2_bias)
    second_low = second.astype(jnp.bfloat16)
    hidden_pre = jnp.dot(second_low, fc1_weight, preferred_element_type=jnp.float32) + fc1_bias
    hidden_low = jax.nn.gelu(hidden_pre, approximate=False).astype(jnp.bfloat16)
    reduce_share = jnp.dot(hidden_low, fc2_weight, preferred_element_type=jnp.float32)
    reduced = lax.psum(reduce_share.astype(jnp.bfloat16), "tensor").astype(jnp.float32) + fc2_bias
    result = after + layer_scale2 * reduced
    block_output = result.astype(jnp.bfloat16).reshape(slots, length, width)
    branch_one = layer_scale1 * attended
    branch_two = layer_scale2 * reduced
    squares = jnp.stack(
        [jnp.sum(live * field * field) for field in (flat, after, result, branch_one, branch_two)]
    )
    count = jnp.sum(validity).astype(jnp.float32)
    square_sums, slot_count = lax.psum((squares, count), "dp")
    grad_rows = cotangent.reshape(rows, width).astype(jnp.float32) * live
    grad_reduced = layer_scale2 * grad_rows
    scale2_grad = jnp.sum(grad_rows * reduced, axis=0)
    second_bias_grad = jnp.sum(grad_reduced, axis=0)
    reduced_low = grad_reduced.astype(jnp.bfloat16)
    second_weight_grad = jnp.einsum(
        "rf,rd->fd", hidden_low, reduced_low, preferred_element_type=jnp.float32
    )
    grad_hidden = jnp.einsum(
        "rd,fd->rf", reduced_low, fc2_weight, preferred_element_type=jnp.float32
    )
    _, gelu_pull = jax.vjp(lambda value: jax.nn.gelu(value, approximate=False), hidden_pre)
    grad_pre = gelu_pull(grad_hidden)[0]
    first_bias_grad = jnp.sum(grad_pre, axis=0)
    pre_low = grad_pre.astype(jnp.bfloat16)
    first_weight_grad = jnp.einsum(
        "rd,rf->df", second_low, pre_low, preferred_element_type=jnp.float32
    )
    second_share = jnp.einsum("rf,df->rd", pre_low, fc1_weight, preferred_element_type=jnp.float32)
    grad_second = lax.psum(second_share.astype(jnp.bfloat16), "tensor").astype(jnp.float32)
    gain2_grad = jnp.sum(grad_second * normed2, axis=0)
    shift2_grad = jnp.sum(grad_second, axis=0)
    grad_after = grad_rows + normalize_back(grad_second, normed2, inverse2, norm2_gain)
    grad_attend = layer_scale1 * grad_after
    scale1_grad = jnp.sum(grad_after * attended, axis=0)
    merge_bias_grad = jnp.sum(grad_attend, axis=0)
    attend_low = grad_attend.astype(jnp.bfloat16)
    merge_weight_grad = jnp.einsum(
        "rn,rd->nd", mixed_rows, attend_low, preferred_element_type=jnp.float32
    )
    grad_mixed = (
        jnp.einsum("rd,nd->rn", attend_low, proj_weight, preferred_element_type=jnp.float32)
        .astype(jnp.bfloat16)
        .reshape(slots, length, local)
    )
    grad_query, grad_key, grad_value = attend_backward(query, keyed, valued, logsums, grad_mixed)
    heads_bias_grad = jnp.stack([jnp.sum(grad_query, axis=0), jnp.sum(grad_value, axis=0)])
    grad_proj = jnp.stack([grad_query, grad_key, grad_value], axis=1).astype(jnp.bfloat16)
    heads_weight_grad = jnp.einsum(
        "rd,rcn->dcn", first_low, grad_proj, preferred_element_type=jnp.float32
    )
    first_share = jnp.einsum(
        "rcn,dcn->rd", grad_proj, qkv_weight, preferred_element_type=jnp.float32
    )
    grad_first = lax.psum(first_share.astype(jnp.bfloat16), "tensor").astype(jnp.float32)
    gain1_grad = jnp.sum(grad_first * normed1, axis=0)
    shift1_grad = jnp.sum(grad_first, axis=0)
    stream_grad = (
        (grad_after + normalize_back(grad_first, normed1, inverse1, norm1_gain))
        .astype(jnp.bfloat16)
        .reshape(slots, length, width)
    )
    (
        gain1_grad,
        shift1_grad,
        heads_weight_grad,
        heads_bias_grad,
        merge_weight_grad,
        merge_bias_grad,
        scale1_grad,
        gain2_grad,
        shift2_grad,
        first_weight_grad,
        first_bias_grad,
        second_weight_grad,
        second_bias_grad,
        scale2_grad,
    ) = (
        lax.psum(gain1_grad.astype(jnp.bfloat16), "dp").astype(jnp.float32),
        lax.psum(shift1_grad.astype(jnp.bfloat16), "dp").astype(jnp.float32),
        lax.psum(heads_weight_grad.astype(jnp.bfloat16), "dp").astype(jnp.float32),
        lax.psum(heads_bias_grad.astype(jnp.bfloat16), "dp").astype(jnp.float32),
        lax.psum(merge_weight_grad.astype(jnp.bfloat16), "dp").astype(jnp.float32),
        lax.psum(merge_bias_grad.astype(jnp.bfloat16), "dp").astype(jnp.float32),
        lax.psum(scale1_grad.astype(jnp.bfloat16), "dp").astype(jnp.float32),
        lax.psum(gain2_grad.astype(jnp.bfloat16), "dp").astype(jnp.float32),
        lax.psum(shift2_grad.astype(jnp.bfloat16), "dp").astype(jnp.float32),
        lax.psum(first_weight_grad.astype(jnp.bfloat16), "dp").astype(jnp.float32),
        lax.psum(first_bias_grad.astype(jnp.bfloat16), "dp").astype(jnp.float32),
        lax.psum(second_weight_grad.astype(jnp.bfloat16), "dp").astype(jnp.float32),
        lax.psum(second_bias_grad.astype(jnp.bfloat16), "dp").astype(jnp.float32),
        lax.psum(scale2_grad.astype(jnp.bfloat16), "dp").astype(jnp.float32),
    )
    root_means = jnp.sqrt(square_sums / (slot_count * SEQ * width))
    return (
        block_output,
        stream_grad,
        gain1_grad,
        shift1_grad,
        heads_weight_grad,
        heads_bias_grad,
        merge_weight_grad,
        merge_bias_grad,
        scale1_grad,
        gain2_grad,
        shift2_grad,
        first_weight_grad,
        first_bias_grad,
        second_weight_grad,
        second_bias_grad,
        scale2_grad,
        root_means,
    )


def solution(mesh):
    return jax.shard_map(
        shards,
        mesh=mesh,
        in_specs=(
            P("dp", None, None),
            P("dp"),
            P(),
            P(),
            P(None, None, "tensor"),
            P(None, "tensor"),
            P("tensor", None),
            P(),
            P(),
            P(),
            P(),
            P(None, "tensor"),
            P("tensor"),
            P("tensor", None),
            P(),
            P(),
            P("dp", None, None),
        ),
        out_specs=(
            P("dp", None, None),
            P("dp", None, None),
            P(),
            P(),
            P(None, None, "tensor"),
            P(None, "tensor"),
            P("tensor", None),
            P(),
            P(),
            P(),
            P(),
            P(None, "tensor"),
            P("tensor"),
            P("tensor", None),
            P(),
            P(),
            P(),
        ),
        check_vma=False,
    )
```

profile of v0, /device:TPU:0, one launch (start us, length us, event | category | flops | bytes accessed | tf_op | source)
XLA Modules:
  0.0 1152.8 jit_solution(1541215123250503405)
XLA Ops:
  12.9 5.8 fusion.117
  28.3 114.0 %while.28 = (s32[]{:T(128)}, bf16[3,1,512,8,64]{2,4,3,1,0:T(8,128)(2,1)}, f32[3,1,8,512]{3,2,1,0:T(8,128)}, s32[3]{0:T(128)S(1)}, bf16[1,1536,8,64]{1,3,2,0:T(8,...) while((s32[]{:T(128)}, ...), condition=%wide.region_5.6_spmd.clone, body=%wide.region_2.5_spmd.clone.sunk | while | flops 1654912512 | bytes 86117592 | solution.py:50
  29.8 13.6 %fusion.160 = (f32[8,512]{1,0:T(8,128)S(1)}, f32[8,512,1536]{2,1,0:T(8,128)}) fusion(bf16[1,1536,8,64]{1,3,2,0:T(8,128)(2,1)} %get-tuple-element.412, bf16[1,1536,8,64]{1,3,2,0:T(8,128)(2,1)} %get-tuple-element.411, s32[]{:T(128)S(6)} %select_n.29, pred[1536]{0:T(1024)(128)(4,1)S(1)} %compare_reduce_fusion.4), kind=kOutput, calls=%fused_computation.166.clone.1 | convolution fusion | flops 824176640 | bytes 27280900 | tf_op jit(solution)/shard_map/while/body/eval_jaxpr/sqhd,skhd->shqk/dot_general | solution.py:39
  43.4 11.4 exponential_reduce_fusion.2
  55.4 11.1 fusion.161
  67.8 13.6 %fusion.160 = (f32[8,512]{1,0:T(8,128)S(1)}, f32[8,512,1536]{2,1,0:T(8,128)}) fusion(bf16[1,1536,8,64]{1,3,2,0:T(8,128)(2,1)} %get-tuple-element.412, bf16[1,1536,8,64]{1,3,2,0:T(8,128)(2,1)} %get-tuple-element.411, s32[]{:T(128)S(6)} %select_n.29, pred[1536]{0:T(1024)(128)(4,1)S(1)} %compare_reduce_fusion.4), kind=kOutput, calls=%fused_computation.166.clone.1 | convolution fusion | flops 824176640 | bytes 27280900 | tf_op jit(solution)/shard_map/while/body/eval_jaxpr/sqhd,skhd->shqk/dot_general | solution.py:39
  81.4 11.4 exponential_reduce_fusion.2
  93.4 11.1 fusion.161
  105.7 13.6 %fusion.160 = (f32[8,512]{1,0:T(8,128)S(1)}, f32[8,512,1536]{2,1,0:T(8,128)}) fusion(bf16[1,1536,8,64]{1,3,2,0:T(8,128)(2,1)} %get-tuple-element.412, bf16[1,1536,8,64]{1,3,2,0:T(8,128)(2,1)} %get-tuple-element.411, s32[]{:T(128)S(6)} %select_n.29, pred[1536]{0:T(1024)(128)(4,1)S(1)} %compare_reduce_fusion.4), kind=kOutput, calls=%fused_computation.166.clone.1 | convolution fusion | flops 824176640 | bytes 27280900 | tf_op jit(solution)/shard_map/while/body/eval_jaxpr/sqhd,skhd->shqk/dot_general | solution.py:39
  119.3 11.4 exponential_reduce_fusion.2
  131.3 11.1 fusion.161
  151.3 88.0 %all-reduce.9.cloned.1.call-done = bf16[1536,1024]{1,0:T(8,128)(2,1)} async-done(((bf16[1536,1024]{1,0:T(8,128)(2,1)}), bf16[1536,1024]{1,0:T(8,128)(2,1)}) %all-reduce.9.cloned.1.call-update) | async-done | bytes 3145744 | tf_op jit(solution)/shard_map/psum | solution.py:145
  246.8 38.1 %multiply_convert_fusion.1 = (bf16[1536,2048]{1,0:T(8,128)(2,1)}, f32[1536,2048]{1,0:T(8,128)}, f32[1536,2048]{1,0:T(8,128)}) fusion(f32[2048]{0:T(1024)S(1)} %copy-done.44, bf16[1024,2048]{1,0:T(8,128)(2,1)S(1)} %copy-done.40, f32[1024]{0:T(1024)S(1)} %copy-done.45, f32[1024]{0:T(1024)S(1)} %copy-done.27, f32[1536]{0:T(1024)S(1)} %add_rsqrt_fusion, ...), kind=kOutput, calls=%fused_computation.53 | convolution fusion | flops 6665797632 | bytes 41979904 | tf_op jit(solution)/shard_map/dot_general | solution.py:149
  284.9 21.6 %fusion.127 = (bf16[2048]{0:T(1024)(128)(2,1)}, bf16[1536,2048]{1,0:T(8,128)(2,1)}) fusion(f32[1536,2048]{1,0:T(8,128)} %get-tuple-element.250, bf16[2048,1024]{1,0:T(8,128)(2,1)} %param.34, bf16[1,1536,1024]{2,1,0:T(8,128)(2,1)} %param.37, f32[1536]{0:T(1024)S(1)} %fusion.113, f32[1024]{0:T(1024)S(1)} %copy-done.36, f32[1536,2048]{1,0:T(8,128)} %get-tuple-element.262, ...), kind=kOutput, calls=%fused_computation.170 | convolution fusion | flops 6499072000 | bytes 38819840 | tf_op jit(solution)/shard_map/rd,fd->rf/dot_general | solution.py:170
  306.5 11.5 convolution_convert_fusion.2
  318.0 8.0 convolution_convert_fusion.3
  326.1 13.3 %convolution_convert_fusion.1 = bf16[1024,2048]{1,0:T(8,128)(2,1)} fusion(bf16[1536,2048]{1,0:T(8,128)(2,1)} %get-tuple-element.264, f32[1024]{0:T(1024)S(1)} %copy-done.45, f32[1024]{0:T(1024)S(1)} %copy-done.27, f32[1536]{0:T(1024)S(1)} %add_rsqrt_fusion, f32[1536]{0:T(1024)S(1)} %broadcast_multiply_fusion.4, f32[1024]{0:T(1024)S(1)} %copy-done.24, ...), kind=kOutput, calls=%fused_computation.129 | convolution fusion | flops 6460276736 | bytes 16805888 | tf_op jit(solution)/shard_map/rd,rf->df/dot_general | solution.py:177
  339.4 140.0 %all-reduce.15.cloned.1.call-done = (bf16[1536,1024]{1,0:T(8,128)(2,1)}, bf16[1536,1024]{1,0:T(8,128)(2,1)}) async-done(((bf16[1536,1024]{1,0:T(8,128)(2,1)}, bf16[1536,1024]{1,0:T(8,128)(2,1)}), (bf16[1536,1024]{1,0:T(8,128)(2,1)}, bf16[1536,1024]{1,0:T(8,128)(2,1)})) %all-reduce.15.cloned.1.call-update) | async-done | bytes 6291472 | tf_op jit(solution)/shard_map/psum | solution.py:152
  479.4 14.5 %fusion.90 = (f32[]{:T(128)}, f32[]{:T(128)}, f32[1536]{0:T(1024)S(1)}, bf16[1024]{0:T(1024)(128)(2,1)}, f32[]{:T(128)}, /*index=5*/f32[]{:T(128)}, bf16[1024]{0...) fusion(bf16[1536,1024]{1,0:T(8,128)(2,1)} %get-tuple-element.244,, ...), kind=kLoop, calls=%fused_computation.106 | loop fusion | flops 62908416 | bytes 18931732 | tf_op jit(solution)/shard_map/reduce_sum | solution.py:158
  494.0 5.7 multiply_reduce_fusion.1
  502.9 265.1 %while.29 = (s32[]{:T(128)}, f32[1,1536,8,64]{1,3,2,0:T(8,128)}, f32[1,1536,8,64]{1,3,2,0:T(8,128)}, f32[3,1,512,8,64]{2,4,3,1,0:T(8,128)}, s32[3]{0:T(128)S(1)}...) while((s32[]{:T(128)}, f32[1,1536,8,64]{1,3,2,0:T(8,128)}, ...), condition=%wide.region_15.16_spmd.clone, body=%wide.region_13.15_spmd.clone.sunk | while | flops 4087346688 | bytes 209276176 | solution.py:97
  507.2 13.3 %fusion.170 = f32[8,512,1536]{2,1,0:T(8,128)} fusion(bf16[1,1536,8,64]{1,3,2,0:T(8,128)(2,1)} %get-tuple-element.457, bf16[1,1536,8,64]{1,3,2,0:T(8,128)(2,1)} %get-tuple-element.456, s32[]{:T(128)S(6)} %select_n.30), kind=kOutput, calls=%fused_computation.28.clone.1 | convolution fusion | flops 805306368 | bytes 27262980 | tf_op jit(solution)/shard_map/while/body/eval_jaxpr/sqhd,skhd->shqk/dot_general | solution.py:74
  520.5 17.4 %multiply_reduce_fusion.5 = (f32[8,512]{1,0:T(8,128)S(1)}, f32[8,512,1536]{2,1,0:T(8,128)}) fusion(f32[8,512,1536]{2,1,0:T(8,128)} %fusion.170, f32[8,512]{1,0:T(8,128)S(1)} %dynamic-slice_bitcast_fusion.2, bf16[1,1536,8,64]{1,3,2,0:T(8,128)(2,1)} %get-tuple-element.454, bf16[1,1536,8,64]{1,3,2,0:T(8,128)(2,1)} %get-tuple-element.453, ...), kind=kOutput, calls=%fused_computation.19.clone.1 | convolution fusion | flops 836759552 | bytes 52463108 | tf_op jit(solution)/shard_map/while/body/eval_jaxpr/sqhd,skhd->shqk/dot_general | solution.py:70
  537.9 21.4 %multiply_convert_fusion.6 = bf16[8,512,1536]{2,1,0:T(8,128)(2,1)} fusion(f32[8,512,1536]{2,1,0:T(8,128)} %get-tuple-element.383, f32[8,512,1536]{2,1,0:T(8,128)} %fusion.170, f32[8,512]{1,0:T(8,128)S(1)} %get-tuple-element.384), kind=kLoop, calls=%fused_computation.18.clone.1 | loop fusion | flops 18874368 | bytes 62930944 | tf_op jit(solution)/shard_map/while/body/eval_jaxpr/convert_element_type | solution.py:78
  559.3 12.4 %fusion.172 = f32[1,1536,8,64]{1,3,2,0:T(8,128)} fusion(f32[8,512,1536]{2,1,0:T(8,128)} %get-tuple-element.383, f32[1,1536,8,64]{1,3,2,0:T(8,128)} %get-tuple-element.435, pred[]{:T(512)S(6)} %compare.3, bf16[1,1536,8,64]{1,3,2,0:T(8,128)(2,1)} %get-tuple-element.456, s32[]{:T(128)S(6)} %select_n.30), kind=kOutput, calls=%fused_computation.27.clone.1 | convolution fusion | flops 813170688 | bytes 31981572 | tf_op jit(solution)/shard_map/while/body/eval_jaxpr/shqk,sqhd->skhd/dot_general | solution.py:88
  571.7 8.7 fusion.171
  580.4 9.9 fusion.173
  594.2 13.3 %fusion.170 = f32[8,512,1536]{2,1,0:T(8,128)} fusion(bf16[1,1536,8,64]{1,3,2,0:T(8,128)(2,1)} %get-tuple-element.457, bf16[1,1536,8,64]{1,3,2,0:T(8,128)(2,1)} %get-tuple-element.456, s32[]{:T(128)S(6)} %select_n.30), kind=kOutput, calls=%fused_computation.28.clone.1 | convolution fusion | flops 805306368 | bytes 27262980 | tf_op jit(solution)/shard_map/while/body/eval_jaxpr/sqhd,skhd->shqk/dot_general | solution.py:74
  607.6 17.4 %multiply_reduce_fusion.5 = (f32[8,512]{1,0:T(8,128)S(1)}, f32[8,512,1536]{2,1,0:T(8,128)}) fusion(f32[8,512,1536]{2,1,0:T(8,128)} %fusion.170, f32[8,512]{1,0:T(8,128)S(1)} %dynamic-slice_bitcast_fusion.2, bf16[1,1536,8,64]{1,3,2,0:T(8,128)(2,1)} %get-tuple-element.454, bf16[1,1536,8,64]{1,3,2,0:T(8,128)(2,1)} %get-tuple-element.453, ...), kind=kOutput, calls=%fused_computation.19.clone.1 | convolution fusion | flops 836759552 | bytes 52463108 | tf_op jit(solution)/shard_map/while/body/eval_jaxpr/sqhd,skhd->shqk/dot_general | solution.py:70
  625.0 21.4 %multiply_convert_fusion.6 = bf16[8,512,1536]{2,1,0:T(8,128)(2,1)} fusion(f32[8,512,1536]{2,1,0:T(8,128)} %get-tuple-element.383, f32[8,512,1536]{2,1,0:T(8,128)} %fusion.170, f32[8,512]{1,0:T(8,128)S(1)} %get-tuple-element.384), kind=kLoop, calls=%fused_computation.18.clone.1 | loop fusion | flops 18874368 | bytes 62930944 | tf_op jit(solution)/shard_map/while/body/eval_jaxpr/convert_element_type | solution.py:78
  646.4 13.3 %fusion.172 = f32[1,1536,8,64]{1,3,2,0:T(8,128)} fusion(f32[8,512,1536]{2,1,0:T(8,128)} %get-tuple-element.383, f32[1,1536,8,64]{1,3,2,0:T(8,128)} %get-tuple-element.435, pred[]{:T(512)S(6)} %compare.3, bf16[1,1536,8,64]{1,3,2,0:T(8,128)(2,1)} %get-tuple-element.456, s32[]{:T(128)S(6)} %select_n.30), kind=kOutput, calls=%fused_computation.27.clone.1 | convolution fusion | flops 813170688 | bytes 31981572 | tf_op jit(solution)/shard_map/while/body/eval_jaxpr/shqk,sqhd->skhd/dot_general | solution.py:88
  659.6 9.6 fusion.171
  669.2 9.8 fusion.173
  683.0 13.3 %fusion.170 = f32[8,512,1536]{2,1,0:T(8,128)} fusion(bf16[1,1536,8,64]{1,3,2,0:T(8,128)(2,1)} %get-tuple-element.457, bf16[1,1536,8,64]{1,3,2,0:T(8,128)(2,1)} %get-tuple-element.456, s32[]{:T(128)S(6)} %select_n.30), kind=kOutput, calls=%fused_computation.28.clone.1 | convolution fusion | flops 805306368 | bytes 27262980 | tf_op jit(solution)/shard_map/while/body/eval_jaxpr/sqhd,skhd->shqk/dot_general | solution.py:74
  696.3 17.4 %multiply_reduce_fusion.5 = (f32[8,512]{1,0:T(8,128)S(1)}, f32[8,512,1536]{2,1,0:T(8,128)}) fusion(f32[8,512,1536]{2,1,0:T(8,128)} %fusion.170, f32[8,512]{1,0:T(8,128)S(1)} %dynamic-slice_bitcast_fusion.2, bf16[1,1536,8,64]{1,3,2,0:T(8,128)(2,1)} %get-tuple-element.454, bf16[1,1536,8,64]{1,3,2,0:T(8,128)(2,1)} %get-tuple-element.453, ...), kind=kOutput, calls=%fused_computation.19.clone.1 | convolution fusion | flops 836759552 | bytes 52463108 | tf_op jit(solution)/shard_map/while/body/eval_jaxpr/sqhd,skhd->shqk/dot_general | solution.py:70
  713.7 21.4 %multiply_convert_fusion.6 = bf16[8,512,1536]{2,1,0:T(8,128)(2,1)} fusion(f32[8,512,1536]{2,1,0:T(8,128)} %get-tuple-element.383, f32[8,512,1536]{2,1,0:T(8,128)} %fusion.170, f32[8,512]{1,0:T(8,128)S(1)} %get-tuple-element.384), kind=kLoop, calls=%fused_computation.18.clone.1 | loop fusion | flops 18874368 | bytes 62930944 | tf_op jit(solution)/shard_map/while/body/eval_jaxpr/convert_element_type | solution.py:78
  735.1 13.3 %fusion.172 = f32[1,1536,8,64]{1,3,2,0:T(8,128)} fusion(f32[8,512,1536]{2,1,0:T(8,128)} %get-tuple-element.383, f32[1,1536,8,64]{1,3,2,0:T(8,128)} %get-tuple-element.435, pred[]{:T(512)S(6)} %compare.3, bf16[1,1536,8,64]{1,3,2,0:T(8,128)(2,1)} %get-tuple-element.456, s32[]{:T(128)S(6)} %select_n.30), kind=kOutput, calls=%fused_computation.27.clone.1 | convolution fusion | flops 813170688 | bytes 31981572 | tf_op jit(solution)/shard_map/while/body/eval_jaxpr/shqk,sqhd->skhd/dot_general | solution.py:88
  748.4 9.6 fusion.171
  757.9 9.8 fusion.173
  795.3 8.8 bitcast_convert_fusion
  804.3 12.1 %convolution_convert_fusion = bf16[2048,1024]{1,0:T(8,128)(2,1)} fusion(bf16[1536,2048]{1,0:T(8,128)(2,1)} %get-tuple-element.249, bf16[1,1536,1024]{2,1,0:T(8,128)(2,1)} %param.37, f32[1536]{0:T(1024)S(1)} %copy-done.21, f32[1024]{0:T(1024)S(1)} %copy-done.37), kind=kOutput, calls=%fused_computation.128 | convolution fusion | flops 6450839552 | bytes 13641728 | tf_op jit(solution)/shard_map/rf,rd->fd/dot_general | solution.py:167
  816.5 5.8 convolution_convert_fusion.7
  822.3 7.6 convolution_convert_fusion.6
  833.3 34.3 %all-reduce = (f32[5]{0:T(128)S(1)}, f32[]{:T(128)}) all-reduce(f32[5]{0:T(128)S(1)} %stack.43, f32[]{:T(128)} %bitcast.19), channel_id=1, replica_groups=mesh['dp'=16,'tensor'=2] {'dp'}, use_global_device_ids=true, to_apply=%region_49.50 | all-reduce | flops 6 | bytes 48 | tf_op jit(solution)/shard_map/psum | solution.py:161
  871.5 18.7 %all-reduce.11.cloned.1.call-done = bf16[1536,1024]{1,0:T(8,128)(2,1)} async-done(((bf16[1536,1024]{1,0:T(8,128)(2,1)}), bf16[1536,1024]{1,0:T(8,128)(2,1)}) %all-reduce.11.cloned.1.call-update) | async-done | bytes 3145744 | tf_op jit(solution)/shard_map/psum | solution.py:206
  897.7 64.4 %all-reduce.1 = (bf16[1024]{0:T(1024)(128)(2,1)S(1)}, bf16[1024]{0:T(1024)(128)(2,1)S(1)}, bf16[2,512]{1,0:T(2,128)(2,1)S(1)}, bf16[1024]{0:T(1024)(128)(2,1)S(1...) all-reduce(bf16[1024]{0:T(1024)(128)(2,1)S(1)} %get-tuple-element.1, ...), channel_id=1, replica_groups=mesh['dp'=16,'tensor'=2] {'dp'}, use_global_device_ids=true, to_apply=%region_20.21 | all-reduce | flops 11264 | bytes 45056 | tf_op jit(solution)/shard_map/psum | solution.py:230
  968.1 7.1 fusion.103
  975.2 153.5 %all-reduce.13.cloned.1.call-done = (bf16[1024,3,512]{2,0,1:T(8,128)(2,1)}, bf16[512,1024]{1,0:T(8,128)(2,1)}, bf16[1024,2048]{1,0:T(8,128)(2,1)}, bf16[2048,1024]{1,0:T(8,128)(2,1)}) async-done(((bf16[1024,3,512]{2,0,1:T(8,128)(2,1)}, bf16[512,1024]{1,0:T(8,128)(2,1)}, bf16[1024,2048]{1,0:T(8,128)(2,1)}, bf16[2048,1024]{1,0:T(8,128)(2,1)}), (bf16[1024,3,512]{2,0,1:T(8,128)(2,1)}, ...) | async-done | bytes 12582928 | tf_op jit(solution)/shard_map/psum | solution.py:232
  (187 shorter events, 106.9 us)
Async XLA Ops:
  7.2 5.7 copy-start
  7.2 5.7 copy-start.28
  7.2 5.7 copy-start.46
  7.2 232.0 %all-reduce.9.cloned.1.call-start = ((), (), s32[]{:S(2)}) async-start(), calls=%async_computation | async-start | bytes 6291456 | tf_op jit(solution)/shard_map/psum | solution.py:145
  7.3 5.6 copy-start.2
  9.8 8.9 copy-start.18
  12.9 5.8 copy-start.22
  43.4 12.0 %copy-start.1 = (bf16[1,1536,8,64]{1,3,2,0:T(8,128)(2,1)S(1)}, bf16[1,1536,8,64]{1,3,2,0:T(8,128)(2,1)}, u32[]{:S(2)}) copy-start(bf16[1,1536,8,64]{1,3,2,0:T(8,128)(2,1)} %get-tuple-element.413) | copy-start | bytes 4718596 | tf_op jit(solution)/shard_map/while
  81.4 12.0 %copy-start.1 = (bf16[1,1536,8,64]{1,3,2,0:T(8,128)(2,1)S(1)}, bf16[1,1536,8,64]{1,3,2,0:T(8,128)(2,1)}, u32[]{:S(2)}) copy-start(bf16[1,1536,8,64]{1,3,2,0:T(8,128)(2,1)} %get-tuple-element.413) | copy-start | bytes 4718596 | tf_op jit(solution)/shard_map/while
  119.3 12.0 %copy-start.1 = (bf16[1,1536,8,64]{1,3,2,0:T(8,128)(2,1)S(1)}, bf16[1,1536,8,64]{1,3,2,0:T(8,128)(2,1)}, u32[]{:S(2)}) copy-start(bf16[1,1536,8,64]{1,3,2,0:T(8,128)(2,1)} %get-tuple-element.413) | copy-start | bytes 4718596 | tf_op jit(solution)/shard_map/while
  147.0 92.2 %copy-start.24 = (f32[1024]{0:T(1024)S(1)}, f32[1024]{0:T(1024)}, u32[]{:S(2)}) copy-start(f32[1024]{0:T(1024)} %param.28) | copy-start | bytes 12292
  147.0 92.2 %copy-start.25 = (f32[1024]{0:T(1024)S(1)}, f32[1024]{0:T(1024)}, u32[]{:S(2)}) copy-start(f32[1024]{0:T(1024)} %param.29) | copy-start | bytes 12292
  150.5 328.9 %all-reduce.15.cloned.1.call-start = ((), (), s32[]{:S(2)}) async-start(), calls=%async_computation.3 | async-start | bytes 12582912 | tf_op jit(solution)/shard_map/psum | solution.py:152
  151.2 342.7 %copy-start.20 = (f32[1536]{0:T(1024)}, f32[1536]{0:T(1024)S(1)}, u32[]{:S(2)}) copy-start(f32[1536]{0:T(1024)S(1)} %fusion.113) | copy-start | bytes 18436
  151.2 95.5 %copy-start.27 = (f32[1024]{0:T(1024)S(1)}, f32[1024]{0:T(1024)}, u32[]{:S(2)}) copy-start(f32[1024]{0:T(1024)} %param.30) | copy-start | bytes 12292
  151.2 95.5 %copy-start.44 = (f32[2048]{0:T(1024)S(1)}, f32[2048]{0:T(1024)}, u32[]{:S(2)}) copy-start(f32[2048]{0:T(1024)} %param.33) | copy-start | bytes 24580
  151.2 95.5 %copy-start.45 = (f32[1024]{0:T(1024)S(1)}, f32[1024]{0:T(1024)}, u32[]{:S(2)}) copy-start(f32[1024]{0:T(1024)} %param.31) | copy-start | bytes 12292
  239.2 7.5 copy-start.40
  246.8 38.1 %copy-start.36 = (f32[1024]{0:T(1024)S(1)}, f32[1024]{0:T(1024)}, u32[]{:S(2)}) copy-start(f32[1024]{0:T(1024)} %param.36) | copy-start | bytes 12292
  306.5 11.5 copy-start.41
  306.5 11.5 copy-start.48
  326.0 564.2 %all-reduce.11.cloned.1.call-start = ((), (), s32[]{:S(2)}) async-start(), calls=%async_computation.1 | async-start | bytes 6291456 | tf_op jit(solution)/shard_map/psum | solution.py:206
  326.1 153.3 %copy-start.35 = (f32[1024]{0:T(1024)S(1)}, f32[1024]{0:T(1024)}, u32[]{:S(2)}) copy-start(f32[1024]{0:T(1024)} %param.35) | copy-start | bytes 12292
  479.4 14.5 %copy-start.4 = (bf16[1,1536,1024]{2,1,0:T(8,128)(2,1)S(1)}, bf16[1,1536,1024]{2,1,0:T(8,128)(2,1)}, u32[]{:S(2)}) copy-start(bf16[1,1536,1024]{2,1,0:T(8,128)(2,1)} %param.21) | copy-start | bytes 9437188
  479.4 14.5 %copy-start.7 = (bf16[1536,1024]{1,0:T(8,128)(2,1)S(1)}, bf16[1536,1024]{1,0:T(8,128)(2,1)}, u32[]{:S(2)}) copy-start(bf16[1536,1024]{1,0:T(8,128)(2,1)} %all-reduce.9.cloned.1.call-done) | copy-start | bytes 9437188
  479.4 14.5 %copy-start.8 = (bf16[1536,1024]{1,0:T(8,128)(2,1)S(1)}, bf16[1536,1024]{1,0:T(8,128)(2,1)}, u32[]{:S(2)}) copy-start(bf16[1536,1024]{1,0:T(8,128)(2,1)} %get-tuple-element.245) | copy-start | bytes 9437188
  479.4 14.5 %copy-start.10 = (bf16[1,1536,1024]{2,1,0:T(8,128)(2,1)S(1)}, bf16[1,1536,1024]{2,1,0:T(8,128)(2,1)}, u32[]{:S(2)}) copy-start(bf16[1,1536,1024]{2,1,0:T(8,128)(2,1)} %param.37) | copy-start | bytes 9437188
  493.9 5.7 copy-start.43
  795.3 8.9 copy-start.21
  795.3 8.9 copy-start.37
  804.2 12.2 %copy-start.26 = (f32[1024]{0:T(1024)S(1)}, f32[1024]{0:T(1024)}, u32[]{:S(2)}) copy-start(f32[1024]{0:T(1024)} %param.29) | copy-start | bytes 12292
  804.2 324.5 %all-reduce.13.cloned.1.call-start = ((), (), s32[]{:S(2)}) async-start(), calls=%async_computation.2 | async-start | bytes 25165824 | tf_op jit(solution)/shard_map/psum | solution.py:232
  804.3 12.1 %copy-start.14 = (bf16[64,8,3,512]{3,1,2,0:T(8,128)(2,1)S(1)}, bf16[64,8,3,512]{3,1,2,0:T(8,128)(2,1)}, u32[]{:S(2)}) copy-start(bf16[64,8,3,512]{3,1,2,0:T(8,128)(2,1)} %copy-done.13) | copy-start | bytes 4718596
  816.4 5.9 copy-start.5
  816.4 5.9 copy-start.15
  816.4 5.9 copy-start.16
  816.4 5.9 copy-start.17
  816.4 5.9 copy-start.19
  816.4 5.9 copy-start.23
  816.4 5.9 copy-start.29
  816.4 5.9 copy-start.47
  867.6 30.1 %copy-start.30 = (bf16[1024]{0:T(1024)(128)(2,1)S(1)}, bf16[1024]{0:T(1024)(128)(2,1)}, u32[]{:S(2)}) copy-start(bf16[1024]{0:T(1024)(128)(2,1)} %get-tuple-element.182) | copy-start | bytes 6148
  867.6 30.1 %copy-start.31 = (bf16[1024]{0:T(1024)(128)(2,1)S(1)}, bf16[1024]{0:T(1024)(128)(2,1)}, u32[]{:S(2)}) copy-start(bf16[1024]{0:T(1024)(128)(2,1)} %get-tuple-element.187) | copy-start | bytes 6148
  867.6 30.1 %copy-start.32 = (bf16[1024]{0:T(1024)(128)(2,1)S(1)}, bf16[1024]{0:T(1024)(128)(2,1)}, u32[]{:S(2)}) copy-start(bf16[1024]{0:T(1024)(128)(2,1)} %get-tuple-element.188) | copy-start | bytes 6148
  867.6 30.1 %copy-start.33 = (bf16[1024]{0:T(1024)(128)(2,1)S(1)}, bf16[1024]{0:T(1024)(128)(2,1)}, u32[]{:S(2)}) copy-start(bf16[1024]{0:T(1024)(128)(2,1)} %get-tuple-element.183) | copy-start | bytes 6148
  867.6 30.1 %copy-start.34 = (bf16[1024]{0:T(1024)(128)(2,1)S(1)}, bf16[1024]{0:T(1024)(128)(2,1)}, u32[]{:S(2)}) copy-start(bf16[1024]{0:T(1024)(128)(2,1)} %get-tuple-element.184) | copy-start | bytes 6148
  867.6 30.1 %copy-start.39 = (bf16[2048]{0:T(1024)(128)(2,1)S(1)}, bf16[2048]{0:T(1024)(128)(2,1)}, u32[]{:S(2)}) copy-start(bf16[2048]{0:T(1024)(128)(2,1)} %get-tuple-element.263) | copy-start | bytes 12292
  1128.7 8.4 copy-start.12
  (7 other events, 25.6 us)
Sparse Core Ops, SparseCore 0:
  150.6 88.5 all-reduce.8
  326.1 153.2 all-reduce.14
  804.3 85.8 all-reduce.10
  895.7 232.9 all-reduce.12
where the time goes:
time: 1160 us; the launch traced here: 1150 us
  matrix products  402 us (35%)
  waiting for transfers between devices  400 us (34%)
  other arithmetic  191 us (16%)
  blocking collectives  98.7 us (9%)
  local copies, waits for them, and re-layouts  34.5 us (3%)
  between operations  15.9 us (1%)
    psum x1, waiting for transfers between devices, shards(): lax.psum(heads_weight_grad.astype(jnp.bfloat16), 'dp').astype(jnp.float32)  153 us
    psum x1, waiting for transfers between devices, shards(): lax.psum(reduce_share.astype(jnp.bfloat16), 'tensor').astype(jnp.float32)  140 us
    dot_general x6, matrix products, one_block(): jnp.einsum('sqhd,skhd->shqk', block, keys, preferred_element_type=jnp.flo...  93 us
    psum x1, waiting for transfers between devices, shards(): lax.psum(attend_share.astype(jnp.bfloat16), 'tensor').astype(jnp.float32)  88 us
    psum x1, blocking collectives, shards(): lax.psum(gain1_grad.astype(jnp.bfloat16), 'dp').astype(jnp.float32)  64.4 us
    convert_element_type x3, other arithmetic, one_block(): dscore_low = dscore.astype(jnp.bfloat16)  64.2 us
    dot_general x3, matrix products, one_block(): jnp.einsum('sqhd,skhd->shqk', grad_block, values, preferred_element_type=...  40 us
    dot_general x3, matrix products, one_block(): jnp.einsum('shqk,sqhd->skhd', probs.astype(jnp.bfloat16), grad_block, pre...  38.9 us
  transfers between devices with their start and end apart: 4, of which 4 were waited for; matrix products, arithmetic and copies ran while one was open for 6% of the time, Pallas kernels for 0%

commit v1 on v0

--- a/solution.py
+++ b/solution.py
@@ -1,6 +1,8 @@
 import jax
 import jax.numpy as jnp
 from jax import lax
+from jax.experimental import pallas as pl
+from jax.experimental.pallas import tpu as pltpu
 from jax.sharding import PartitionSpec as P
 
 HEAD_DIM = 64
@@ -26,83 +28,95 @@
     return inverse * (centered - normed * jnp.mean(scaled * normed, axis=-1, keepdims=True))
 
 
-def attend_forward(query, keyed, valued):
-    slots, length, width = query.shape
-    heads = width // HEAD_DIM
-    queries = query.reshape(slots, length, heads, HEAD_DIM)
-    keys = keyed.reshape(slots, length, heads, HEAD_DIM)
-    values = valued.reshape(slots, length, heads, HEAD_DIM)
-    live = (jnp.arange(length) < SEQ)[None, None, None, :]
-
-    def one_block(index):
-        block = lax.dynamic_slice_in_dim(queries, index * PAD_UNIT, PAD_UNIT, 1)
-        scores = jnp.einsum(
-            "sqhd,skhd->shqk", block, keys, preferred_element_type=jnp.float32
-        ) * HEAD_DIM ** (-0.5)
-        scores = jnp.where(live, scores, -1e30)
-        top = jnp.max(scores, axis=-1, keepdims=True)
-        total = jnp.sum(jnp.exp(scores - top), axis=-1, keepdims=True)
-        logsum = top + jnp.log(total)
-        probs = jnp.exp(scores - logsum).astype(jnp.bfloat16)
-        mixed = jnp.einsum("shqk,skhd->sqhd", probs, values, preferred_element_type=jnp.float32)
-        return (mixed.astype(jnp.bfloat16), logsum[..., 0])
-
-    mixed, logsums = lax.map(one_block, jnp.arange(length // PAD_UNIT))
-    mixed = mixed.transpose(1, 0, 2, 3, 4).reshape(slots, length, width)
-    return (mixed, logsums)
-
-
-def attend_backward(query, keyed, valued, logsums, grad_mixed):
-    slots, length, width = query.shape
-    heads = width // HEAD_DIM
-    queries = query.reshape(slots, length, heads, HEAD_DIM)
-    keys = keyed.reshape(slots, length, heads, HEAD_DIM)
-    values = valued.reshape(slots, length, heads, HEAD_DIM)
-    grads = grad_mixed.reshape(slots, length, heads, HEAD_DIM)
-    live = (jnp.arange(length) < SEQ)[None, None, None, :]
-    factor = HEAD_DIM ** (-0.5)
-
-    def one_block(carry, index):
-        key_acc, value_acc = carry
-        block = lax.dynamic_slice_in_dim(queries, index * PAD_UNIT, PAD_UNIT, 1)
-        grad_block = lax.dynamic_slice_in_dim(grads, index * PAD_UNIT, PAD_UNIT, 1)
-        scores = (
-            jnp.einsum("sqhd,skhd->shqk", block, keys, preferred_element_type=jnp.float32) * factor
-        )
-        scores = jnp.where(live, scores, -1e30)
-        probs = jnp.exp(scores - logsums[index][..., None])
-        dprob = jnp.einsum(
-            "sqhd,skhd->shqk", grad_block, values, preferred_element_type=jnp.float32
-        )
-        dscore = probs * (dprob - jnp.sum(probs * dprob, axis=-1, keepdims=True))
-        dscore_low = dscore.astype(jnp.bfloat16)
-        dquery = (
-            jnp.einsum("shqk,skhd->sqhd", dscore_low, keys, preferred_element_type=jnp.float32)
-            * factor
-        )
-        key_acc = (
-            key_acc
-            + jnp.einsum("shqk,sqhd->skhd", dscore_low, block, preferred_element_type=jnp.float32)
-            * factor
-        )
-        value_acc = value_acc + jnp.einsum(
-            "shqk,sqhd->skhd",
-            probs.astype(jnp.bfloat16),
-            grad_block,
-            preferred_element_type=jnp.float32,
-        )
-        return ((key_acc, value_acc), dquery)
-
-    empty = jnp.zeros((slots, length, heads, HEAD_DIM), jnp.float32)
-    (grad_key, grad_value), grad_query = lax.scan(
-        one_block, (empty, empty), jnp.arange(length // PAD_UNIT)
-    )
-    grad_query = grad_query.transpose(1, 0, 2, 3, 4).reshape(slots * length, width)
-    return (
-        grad_query,
-        grad_key.reshape(slots * length, width),
-        grad_value.reshape(slots * length, width),
-    )
+NT=(((1,),(1,)),((),()))
+NN=(((1,),(0,)),((),()))
+def chunks_of(n,b):
+    return [(i,min(b,n-i)) for i in range(0,n,b)]
+def attn_fwd(q,k,v,bq=256):
+    L,W=q.shape; pairs=W//128; KL=-(-SEQ//16)*16
+    def kern(q_ref,k_ref,v_ref,o_ref,lse_ref,kh_ref,vt_ref):
+        lane=lax.broadcasted_iota(jnp.int32,(1,128),1)
+        row=lax.broadcasted_iota(jnp.int32,(KL,128),0)
+        k2=k_ref[:KL,:]; v2=v_ref[:KL,:]
+        for h in range(2):
+            mine=(lane//64)==h
+            spare=lane==(64*(1-h))
+            pad=jnp.where((row>=SEQ)&spare,-1e30,0.0).astype(jnp.bfloat16)
+            kh_ref[h]=jnp.where(mine,k2,pad)
+        vt=v2.T
+        ones=jnp.ones((16,KL),jnp.bfloat16)
+        for h in range(2):
+            vt_ref[h]=jnp.concatenate([vt[h*64:(h+1)*64],ones],axis=0)
+        for (s0,b) in chunks_of(L,bq):
+            q2=q_ref[s0:s0+b,:]
+            outs=[]
+            for h in range(2):
+                mine=(lane//64)==h
+                spare=lane==(64*(1-h))
+                qh=jnp.where(mine,q2,jnp.where(spare,1.0,0.0).astype(jnp.bfloat16))
+                sT=lax.dot_general(kh_ref[h],qh,NT,preferred_element_type=jnp.float32)
+                m=jnp.max(sT,axis=0,keepdims=True)
+                pT=jnp.exp(sT-m).astype(jnp.bfloat16)
+                acc=lax.dot_general(vt_ref[h],pT,NN,preferred_element_type=jnp.float32)
+                l=acc[64:65,:]
+                outs.append(acc[:64]*(1.0/l))
+                lse_ref[0,h:h+1,s0:s0+b]=m+jnp.log(l)
+            o_ref[s0:s0+b,:]=jnp.concatenate(outs,axis=0).T.astype(jnp.bfloat16)
+    spec=pl.BlockSpec((L,128),lambda p:(0,p))
+    return pl.pallas_call(kern,grid=(pairs,),in_specs=[spec]*3,
+        out_specs=[spec,pl.BlockSpec((1,8,L),lambda p:(p,0,0))],
+        out_shape=[jax.ShapeDtypeStruct((L,W),jnp.bfloat16),jax.ShapeDtypeStruct((pairs,8,L),jnp.float32)],
+        scratch_shapes=[pltpu.VMEM((2,KL,128),jnp.bfloat16),pltpu.VMEM((2,80,KL),jnp.bfloat16)],
+        compiler_params=pltpu.CompilerParams(vmem_limit_bytes=56<<20),name="attend_fwd")(q,k,v)
+def attn_bwd(q,k,v,o,do,lse,bq=256):
+    L,W=q.shape; pairs=W//128; KL=-(-SEQ//16)*16; QL=-(-SEQ//128)*128
+    def kern(q_ref,k_ref,v_ref,o_ref,do_ref,lse_ref,dq_ref,dk_ref,dv_ref,kh_ref,vh_ref,kt_ref,dk_acc,dv_acc):
+        lane=lax.broadcasted_iota(jnp.int32,(1,128),1)
+        row=lax.broadcasted_iota(jnp.int32,(KL,128),0)
+        zero=jnp.zeros((),jnp.bfloat16)
+        k2=k_ref[:KL,:]; v2=v_ref[:KL,:]
+        for h in range(2):
+            mine=(lane//64)==h
+            spare=lane==(64*(1-h))
+            pad=jnp.where((row>=SEQ)&spare,-1e30,0.0).astype(jnp.bfloat16)
+            kh_ref[h]=jnp.where(mine,k2,pad)
+            vh_ref[h]=jnp.where(mine,v2,zero)
+        kt_ref[...]=k2.T
+        for ci,(s0,b) in enumerate(chunks_of(QL,bq)):
+            q2=q_ref[s0:s0+b,:]; do2=do_ref[s0:s0+b,:]
+            prod=(do2.astype(jnp.float32)*o_ref[s0:s0+b,:].astype(jnp.float32)).T
+            dqs=[]; dk=None; dv=None
+            for h in range(2):
+                mine=(lane//64)==h
+                spare=lane==(64*(1-h))
+                delta=jnp.sum(prod[h*64:(h+1)*64],axis=0,keepdims=True)
+                qz=jnp.where(mine,q2,zero); doz=jnp.where(mine,do2,zero)
+                qh=jnp.where(mine,q2,jnp.where(spare,1.0,0.0).astype(jnp.bfloat16))
+                sT=lax.dot_general(kh_ref[h],qh,NT,preferred_element_type=jnp.float32)
+                pT=jnp.exp(sT-lse_ref[0,h:h+1,s0:s0+b])
+                dpT=lax.dot_general(vh_ref[h],do2,NT,preferred_element_type=jnp.float32)
+                ds=(pT*(dpT-delta)).astype(jnp.bfloat16)
+                pb=pT.astype(jnp.bfloat16)
+                dvh=lax.dot_general(pb,doz,NN,preferred_element_type=jnp.float32)
+                dkh=lax.dot_general(ds,qz,NN,preferred_element_type=jnp.float32)
+                dv=dvh if dv is None else dv+dvh
+                dk=dkh if dk is None else dk+dkh
+                dqs.append(lax.dot_general(kt_ref[h*64:(h+1)*64,:],ds,NN,preferred_element_type=jnp.float32))
+            if ci==0:
+                dk_acc[...]=dk; dv_acc[...]=dv
+            else:
+                dk_acc[...]+=dk; dv_acc[...]+=dv
+            dq_ref[s0:s0+b,:]=(jnp.concatenate(dqs,axis=0).T*HEAD_DIM**-0.5).astype(dq_ref.dtype)
+        dk_ref[:KL,:]=dk_acc[...].astype(dk_ref.dtype); dv_ref[:KL,:]=dv_acc[...].astype(dv_ref.dtype)
+        if KL<QL:
+            dk_ref[KL:,:]=jnp.zeros((QL-KL,128),dk_ref.dtype); dv_ref[KL:,:]=jnp.zeros((QL-KL,128),dv_ref.dtype)
+    spec=pl.BlockSpec((L,128),lambda p:(0,p))
+    ospec=pl.BlockSpec((QL,128),lambda p:(0,p))
+    return pl.pallas_call(kern,grid=(pairs,),in_specs=[spec]*5+[pl.BlockSpec((1,8,L),lambda p:(p,0,0))],
+        out_specs=[ospec]*3,
+        out_shape=[jax.ShapeDtypeStruct((QL,W),jnp.bfloat16)]*3,
+        scratch_shapes=[pltpu.VMEM((2,KL,128),jnp.bfloat16),pltpu.VMEM((2,KL,128),jnp.bfloat16),pltpu.VMEM((128,KL),jnp.bfloat16),pltpu.VMEM((KL,128),jnp.float32),pltpu.VMEM((KL,128),jnp.float32)],
+        compiler_params=pltpu.CompilerParams(vmem_limit_bytes=56<<20),name="attend_bwd")(q,k,v,o,do,lse)
 
 
 def shards(
@@ -136,11 +150,10 @@
     first, normed1, inverse1 = normalize(flat, norm1_gain, norm1_bias)
     first_low = first.astype(jnp.bfloat16)
     projected = jnp.einsum("rd,dcn->rcn", first_low, qkv_weight, preferred_element_type=jnp.float32)
-    query = (projected[:, 0] + qkv_bias[0]).astype(jnp.bfloat16).reshape(slots, length, local)
-    keyed = projected[:, 1].astype(jnp.bfloat16).reshape(slots, length, local)
-    valued = (projected[:, 2] + qkv_bias[1]).astype(jnp.bfloat16).reshape(slots, length, local)
-    mixed, logsums = attend_forward(query, keyed, valued)
-    mixed_rows = mixed.reshape(rows, local)
+    query = ((projected[:, 0] + qkv_bias[0]) * HEAD_DIM**-0.5).astype(jnp.bfloat16)
+    keyed = projected[:, 1].astype(jnp.bfloat16)
+    valued = (projected[:, 2] + qkv_bias[1]).astype(jnp.bfloat16)
+    mixed_rows, logsums = attn_fwd(query, keyed, valued, 512)
     attend_share = jnp.dot(mixed_rows, proj_weight, preferred_element_type=jnp.float32)
     attended = lax.psum(attend_share.astype(jnp.bfloat16), "tensor").astype(jnp.float32) + proj_bias
     after = flat + layer_scale1 * attended
@@ -189,21 +202,23 @@
     merge_weight_grad = jnp.einsum(
         "rn,rd->nd", mixed_rows, attend_low, preferred_element_type=jnp.float32
     )
-    grad_mixed = (
-        jnp.einsum("rd,nd->rn", attend_low, proj_weight, preferred_element_type=jnp.float32)
-        .astype(jnp.bfloat16)
-        .reshape(slots, length, local)
-    )
-    grad_query, grad_key, grad_value = attend_backward(query, keyed, valued, logsums, grad_mixed)
-    heads_bias_grad = jnp.stack([jnp.sum(grad_query, axis=0), jnp.sum(grad_value, axis=0)])
+    grad_mixed = jnp.einsum(
+        "rd,nd->rn", attend_low, proj_weight, preferred_element_type=jnp.float32
+    ).astype(jnp.bfloat16)
+    grad_query, grad_key, grad_value = attn_bwd(
+        query, keyed, valued, mixed_rows, grad_mixed, logsums, 256
+    )
+    some = grad_query.shape[0]
+    heads_bias_grad = jnp.stack([jnp.sum(grad_query.astype(jnp.float32), axis=0), jnp.sum(grad_value.astype(jnp.float32), axis=0)])
     grad_proj = jnp.stack([grad_query, grad_key, grad_value], axis=1).astype(jnp.bfloat16)
     heads_weight_grad = jnp.einsum(
-        "rd,rcn->dcn", first_low, grad_proj, preferred_element_type=jnp.float32
+        "rd,rcn->dcn", first_low[:some], grad_proj, preferred_element_type=jnp.float32
     )
     first_share = jnp.einsum(
         "rcn,dcn->rd", grad_proj, qkv_weight, preferred_element_type=jnp.float32
     )
     grad_first = lax.psum(first_share.astype(jnp.bfloat16), "tensor").astype(jnp.float32)
+    grad_first = jnp.pad(grad_first, ((0, rows - some), (0, 0)))
     gain1_grad = jnp.sum(grad_first * normed1, axis=0)
     shift1_grad = jnp.sum(grad_first, axis=0)
     stream_grad = (

time: 1160 us -> 812 us (0.70)
  matrix products: 402 us -> 138 us
  other arithmetic: 191 us -> 79.9 us
  Pallas kernels: 0 us -> 73.6 us
  local copies, waits for them, and re-layouts: 34.5 us -> 6.66 us
    dot_general x22 -> x1, matrix products: 270 us -> 6.61 us  [shards(): jnp.einsum('rd,rcn->dcn', first_low[:some], grad_proj, preferred_element_...]
    pallas_call x0 -> x2, Pallas kernels: none -> 73.6 us  [the longest x1 43 us: attn_bwd(): pl.pallas_call(kern, grid=(pairs,), in_specs=[spec] * 5 + [pl.BlockSpec((...]
    convert_element_type x4 -> x2, other arithmetic: 69.1 us -> 4.11 us  [the longest x1 2.65 us: shards(): valued = (projected[:, 2] + qkv_bias[1]).astype(jnp.bfloat16)]
    reduce_sum x5 -> x2, other arithmetic: 42.8 us -> 3.25 us  [the longest x1 1.62 us: shards(): jnp.sum(grad_query.astype(jnp.float32), axis=0)]
    another operation x6 -> x2, local copies, waits for them, and re-layouts: 15.7 us -> 0.01 us  [shards(): jnp.stack([jnp.sum(grad_query.astype(jnp.float32), axis=0), jnp.sum(grad_...]
  transfers between devices with their start and end apart: 4 -> 4, of which waited for: 4 -> 4; matrix products, arithmetic and copies ran while one was open for 6% -> 8% of each run, Pallas kernels for 0% -> 0%
where the time goes in v1:
time: 812 us; the launch traced here: 806 us
  waiting for transfers between devices  393 us (48%)
  matrix products  138 us (17%)
  blocking collectives  98.9 us (12%)
  other arithmetic  79.9 us (10%)
  Pallas kernels  73.6 us (9%)
  between operations  15.8 us (2%)
    psum x1, waiting for transfers between devices, shards(): lax.psum(heads_weight_grad.astype(jnp.bfloat16), 'dp').astype(jnp.float32)  153 us
    psum x1, waiting for transfers between devices, shards(): lax.psum(reduce_share.astype(jnp.bfloat16), 'tensor').astype(jnp.float32)  140 us
    psum x1, waiting for transfers between devices, shards(): lax.psum(attend_share.astype(jnp.bfloat16), 'tensor').astype(jnp.float32)  88 us
    psum x1, blocking collectives, shards(): lax.psum(gain1_grad.astype(jnp.bfloat16), 'dp').astype(jnp.float32)  64.8 us
    pallas_call x1, Pallas kernels, attn_bwd(): pl.pallas_call(kern, grid=(pairs,), in_specs=[spec] * 5 + [pl.BlockSpec((...  43 us
    dot_general x1, matrix products, shards(): jnp.dot(second_low, fc1_weight, preferred_element_type=jnp.float32)  38.1 us
    psum x1, blocking collectives, shards(): square_sums, slot_count = lax.psum((squares, count), 'dp')  34.1 us
    pallas_call x1, Pallas kernels, attn_fwd(): pl.pallas_call(kern, grid=(pairs,), in_specs=[spec] * 3, out_specs=[spec,...  30.7 us
  transfers between devices with their start and end apart: 4, of which 4 were waited for; matrix products, arithmetic and copies ran while one was open for 8% of the time, Pallas kernels for 0%

profile of v1, /device:TPU:0, one launch (start us, length us, event | category | flops | bytes accessed | tf_op | source)
XLA Modules:
  0.0 805.9 jit_solution(1751091993385710526)
XLA Ops:
  7.3 0.9 fusion.73
  8.1 2.6 convert_reduce_fusion
  10.8 2.9 fusion.24
  14.2 1.5 fusion.19
  15.7 5.1 fusion.53
  20.9 1.3 fusion.59.k_ref
  22.2 2.7 fusion.49
  24.9 30.7 %attend_fwd.1 = (bf16[1536,512]{1,0:T(8,128)(2,1)}, f32[4,8,1536]{2,1,0:T(8,128)}) custom-call(bf16[1536,512]{1,0:T(8,128)(2,1)} %get-tuple-element.67.q_ref, bf16[1536,512]{1,0:T(8,128)(2,1)} %fusion.59.k_ref, bf16[1536,512]{1,0:T(8,128)(2,1)} %get-tuple-element.66.v_ref), custom_call_target="tpu_custom_call" | custom-call | tf_op jit(solution)/shard_map/attend_fwd/pallas_call | solution.py:66
  55.6 4.9 convolution_convert_fusion.4
  61.2 88.0 %all-reduce.10.cloned.1.call-done = bf16[1536,1024]{1,0:T(8,128)(2,1)} async-done(((bf16[1536,1024]{1,0:T(8,128)(2,1)}), bf16[1536,1024]{1,0:T(8,128)(2,1)}) %all-reduce.10.cloned.1.call-update) | async-done | bytes 3145744 | tf_op jit(solution)/shard_map/psum | solution.py:158
  149.2 4.3 fusion.69
  153.9 2.6 multiply_reduce_fusion.1
  156.6 38.1 %multiply_convert_fusion = (bf16[1536,2048]{1,0:T(8,128)(2,1)}, f32[1536,2048]{1,0:T(8,128)}, f32[1536,2048]{1,0:T(8,128)}) fusion(f32[2048]{0:T(1024)S(1)} %copy-done.33, bf16[1024,2048]{1,0:T(8,128)(2,1)S(1)} %copy-done.28, f32[1024]{0:T(1024)S(1)} %copy-done.34, f32[1024]{0:T(1024)S(1)} %copy-done.24, f32[1536]{0:T(1024)S(1)} %add_rsqrt_fusion, ...), kind=kOutput, calls=%fused_computation.3 | convolution fusion | flops 6665797632 | bytes 41979904 | tf_op jit(solution)/shard_map/dot_general | solution.py:162
  194.6 20.9 %fusion.74 = (bf16[2048]{0:T(1024)(128)(2,1)S(1)}, bf16[1536,2048]{1,0:T(8,128)(2,1)}) fusion(f32[1536,2048]{1,0:T(8,128)} %get-tuple-element.64, bf16[2048,1024]{1,0:T(8,128)(2,1)} %param.30, bf16[1,1536,1024]{2,1,0:T(8,128)(2,1)} %param.33, f32[1536]{0:T(1024)S(1)} %fusion.66, f32[1024]{0:T(1024)S(1)} %copy-done.27, f32[1536,2048]{1,0:T(8,128)} %get-tuple-element.70, ...), kind=kOutput, calls=%fused_computation.124 | convolution fusion | flops 6499072000 | bytes 38819840 | tf_op jit(solution)/shard_map/rd,fd->rf/dot_general | solution.py:183
  215.6 11.9 %convolution_convert_fusion.2 = bf16[1536,1024]{1,0:T(8,128)(2,1)} fusion(bf16[1024,2048]{1,0:T(8,128)(2,1)} %param.28, bf16[1536,2048]{1,0:T(8,128)(2,1)} %get-tuple-element.72), kind=kOutput, calls=%fused_computation.80 | convolution fusion | flops 6444023808 | bytes 13631488 | tf_op jit(solution)/shard_map/rf,df->rd/dot_general | solution.py:193
  227.5 8.0 convolution_convert_fusion.3
  235.6 13.3 %convolution_convert_fusion.1 = bf16[1024,2048]{1,0:T(8,128)(2,1)} fusion(bf16[1536,2048]{1,0:T(8,128)(2,1)} %get-tuple-element.72, f32[1024]{0:T(1024)S(1)} %copy-done.34, f32[1024]{0:T(1024)S(1)} %copy-done.24, f32[1536]{0:T(1024)S(1)} %add_rsqrt_fusion, f32[1536]{0:T(1024)S(1)} %broadcast_multiply_fusion.4, f32[1024]{0:T(1024)S(1)} %copy-done.20, ...), kind=kOutput, calls=%fused_computation.79 | convolution fusion | flops 6460276736 | bytes 16805888 | tf_op jit(solution)/shard_map/rd,rf->df/dot_general | solution.py:190
  248.9 140.1 %all-reduce.16.cloned.1.call-done = (bf16[1536,1024]{1,0:T(8,128)(2,1)}, bf16[1536,1024]{1,0:T(8,128)(2,1)}) async-done(((bf16[1536,1024]{1,0:T(8,128)(2,1)}, bf16[1536,1024]{1,0:T(8,128)(2,1)}), (bf16[1536,1024]{1,0:T(8,128)(2,1)}, bf16[1536,1024]{1,0:T(8,128)(2,1)})) %all-reduce.16.cloned.1.call-update) | async-done | bytes 6291472 | tf_op jit(solution)/shard_map/psum | solution.py:165
  388.9 14.4 %fusion.34 = (f32[]{:T(128)}, f32[]{:T(128)}, f32[1536]{0:T(1024)S(1)}, bf16[1024]{0:T(1024)(128)(2,1)S(1)}, f32[]{:T(128)}, /*index=5*/f32[]{:T(128)}, bf16[102...) fusion(bf16[1536,1024]{1,0:T(8,128)(2,1)} %get-tuple-element.60, ...), kind=kLoop, calls=%fused_computation.56 | loop fusion | flops 62908416 | bytes 18931732 | tf_op jit(solution)/shard_map/reduce_sum | solution.py:171
  403.4 5.1 multiply_reduce_fusion
  408.5 3.2 convolution_convert_fusion.5.do_ref
  411.7 43.0 %attend_bwd.1 = (bf16[1408,512]{1,0:T(8,128)(2,1)}, bf16[1408,512]{1,0:T(8,128)(2,1)}, bf16[1408,512]{1,0:T(8,128)(2,1)}) custom-call(bf16[1536,512]{1,0:T(8,128)(2,1)} %get-tuple-element.67.q_ref, bf16[1536,512]{1,0:T(8,128)(2,1)} %fusion.59.k_ref, bf16[1536,512]{1,0:T(8,128)(2,1)} %get-tuple-element.66.v_ref, bf16[1536,512]{1,0:T(8,128)(2,1)} %get-tuple-element.22.o_ref, ...), custom_call_target="tpu_custom_call" | custom-call | tf_op jit(solution)/shard_map/attend_bwd/pallas_call | solution.py:115
  454.7 8.3 %bitcast_convert_fusion = bf16[1408,1024]{1,0:T(8,128)(2,1)} fusion(bf16[1024,3,512]{2,0,1:T(8,128)(2,1)S(1)} %copy-done, bf16[1408,1,512]{2,0,1:T(8,128)(2,1)} %bitcast.134, bf16[1408,1,512]{2,0,1:T(8,128)(2,1)} %bitcast.140, bf16[1408,1,512]{2,0,1:T(8,128)(2,1)} %bitcast.136), kind=kOutput, calls=%fused_computation.76 | convolution fusion | flops 4434952192 | bytes 10354688 | tf_op jit(solution)/shard_map/rcn,dcn->rd/dot_general | solution.py:217
  463.1 12.3 %convolution_convert_fusion = bf16[2048,1024]{1,0:T(8,128)(2,1)} fusion(bf16[1536,2048]{1,0:T(8,128)(2,1)} %get-tuple-element.63, bf16[1,1536,1024]{2,1,0:T(8,128)(2,1)} %param.33, f32[1536]{0:T(1024)S(1)} %fusion.66, f32[1024]{0:T(1024)S(1)} %copy-done.27), kind=kOutput, calls=%fused_computation.78 | convolution fusion | flops 6450839552 | bytes 13641728 | tf_op jit(solution)/shard_map/rf,rd->fd/dot_general | solution.py:180
  475.4 5.8 convolution_convert_fusion.6
  481.2 6.6 fusion.58
  487.9 3.3 stack.54
  491.2 34.1 %all-reduce.1 = (f32[5]{0:T(128)S(1)}, f32[]{:T(128)}) all-reduce(f32[5]{0:T(128)S(1)} %stack.54, f32[]{:T(128)} %bitcast.21), channel_id=1, replica_groups=mesh['dp'=16,'tensor'=2] {'dp'}, use_global_device_ids=true, to_apply=%region_42.43 | all-reduce | flops 6 | bytes 48 | tf_op jit(solution)/shard_map/psum | solution.py:174
  525.3 2.5 reduce_sum.238
  527.7 1.6 reduce.3
  529.4 1.6 reduce.4
  532.2 11.1 %all-reduce.12.cloned.1.call-done = bf16[1408,1024]{1,0:T(8,128)(2,1)} async-done(((bf16[1408,1024]{1,0:T(8,128)(2,1)}), bf16[1408,1024]{1,0:T(8,128)(2,1)}) %all-reduce.12.cloned.1.call-update) | async-done | bytes 2883600 | tf_op jit(solution)/shard_map/psum | solution.py:220
  543.3 2.3 pad_reduce_fusion
  545.6 5.0 fusion.31
  550.6 64.8 %all-reduce.2 = (bf16[1024]{0:T(1024)(128)(2,1)S(1)}, bf16[1024]{0:T(1024)(128)(2,1)S(1)}, bf16[2,512]{1,0:T(2,128)(2,1)S(1)}, bf16[1024]{0:T(1024)(128)(2,1)S(1...) all-reduce(bf16[1024]{0:T(1024)(128)(2,1)S(1)} %get-tuple-element.3, ...), channel_id=1, replica_groups=mesh['dp'=16,'tensor'=2] {'dp'}, use_global_device_ids=true, to_apply=%region_13.0 | all-reduce | flops 11264 | bytes 45056 | tf_op jit(solution)/shard_map/psum | solution.py:245
  615.4 0.6 convert_element_type.198
  616.6 0.6 convert_element_type.205
  618.4 0.6 convert_element_type.213
  619.0 0.6 convert_element_type.214
  619.5 0.6 convert_element_type.222
  620.1 0.6 convert_element_type.224
  620.7 0.6 convert_element_type.218
  621.3 7.1 fusion.47
  628.4 153.4 %all-reduce.14.cloned.1.call-done = (bf16[1024,3,512]{2,0,1:T(8,128)(2,1)}, bf16[512,1024]{1,0:T(8,128)(2,1)}, bf16[1024,2048]{1,0:T(8,128)(2,1)}, bf16[2048,1024]{1,0:T(8,128)(2,1)}) async-done(((bf16[1024,3,512]{2,0,1:T(8,128)(2,1)}, bf16[512,1024]{1,0:T(8,128)(2,1)}, bf16[1024,2048]{1,0:T(8,128)(2,1)}, bf16[2048,1024]{1,0:T(8,128)(2,1)}), (bf16[1024,3,512]{2,0,1:T(8,128)(2,1)}, ...) | async-done | bytes 12582928 | tf_op jit(solution)/shard_map/psum | solution.py:247
  781.8 2.9 convert_element_type.207
  784.7 5.5 convert_element_type.202
  790.2 4.4 convert_element_type.216
  794.7 4.4 convert_element_type.220
  (95 shorter events, 3.7 us)
Async XLA Ops:
  7.2 8.5 %copy-start = (bf16[1024,3,512]{2,0,1:T(8,128)(2,1)S(1)}, bf16[1024,3,512]{2,0,1:T(8,128)(2,1)}, u32[]{:S(2)}) copy-start(bf16[1024,3,512]{2,0,1:T(8,128)(2,1)} %param.21) | copy-start | bytes 9437188
  7.2 7.0 copy-start.22
  7.2 7.0 copy-start.25
  7.2 142.0 %all-reduce.10.cloned.1.call-start = ((), (), s32[]{:S(2)}) async-start(), calls=%async_computation | async-start | bytes 6291456 | tf_op jit(solution)/shard_map/psum | solution.py:158
  7.3 7.0 copy-start.1
  10.7 2.9 copy-start.16
  13.6 0.6 copy-start.18
  15.7 5.2 copy-start.11
  22.2 33.3 %copy-start.31 = (bf16[512,1024]{1,0:T(8,128)(2,1)S(1)}, bf16[512,1024]{1,0:T(8,128)(2,1)}, u32[]{:S(2)}) copy-start(bf16[512,1024]{1,0:T(8,128)(2,1)} %param.23) | copy-start | bytes 3145732
  55.5 93.6 %copy-start.20 = (f32[1024]{0:T(1024)S(1)}, f32[1024]{0:T(1024)}, u32[]{:S(2)}) copy-start(f32[1024]{0:T(1024)} %param.24) | copy-start | bytes 12292
  55.6 93.6 %copy-start.21 = (f32[1024]{0:T(1024)S(1)}, f32[1024]{0:T(1024)}, u32[]{:S(2)}) copy-start(f32[1024]{0:T(1024)} %param.25) | copy-start | bytes 12292
  60.5 328.4 %all-reduce.16.cloned.1.call-start = ((), (), s32[]{:S(2)}) async-start(), calls=%async_computation.3 | async-start | bytes 12582912 | tf_op jit(solution)/shard_map/psum | solution.py:165
  61.2 95.3 %copy-start.24 = (f32[1024]{0:T(1024)S(1)}, f32[1024]{0:T(1024)}, u32[]{:S(2)}) copy-start(f32[1024]{0:T(1024)} %param.26) | copy-start | bytes 12292
  61.2 95.3 %copy-start.33 = (f32[2048]{0:T(1024)S(1)}, f32[2048]{0:T(1024)}, u32[]{:S(2)}) copy-start(f32[2048]{0:T(1024)} %param.29) | copy-start | bytes 24580
  61.2 95.3 %copy-start.34 = (f32[1024]{0:T(1024)S(1)}, f32[1024]{0:T(1024)}, u32[]{:S(2)}) copy-start(f32[1024]{0:T(1024)} %param.27) | copy-start | bytes 12292
  149.2 4.3 copy-start.2
  149.2 4.7 copy-start.4
  149.2 7.3 copy-start.28
  156.5 38.1 %copy-start.27 = (f32[1024]{0:T(1024)S(1)}, f32[1024]{0:T(1024)}, u32[]{:S(2)}) copy-start(f32[1024]{0:T(1024)} %param.32) | copy-start | bytes 12292
  215.6 11.9 %copy-start.29 = (bf16[2048,1024]{1,0:T(8,128)(2,1)S(1)}, bf16[2048,1024]{1,0:T(8,128)(2,1)}, u32[]{:S(2)}) copy-start(bf16[2048,1024]{1,0:T(8,128)(2,1)} %param.30) | copy-start | bytes 12582916
  215.6 11.9 %copy-start.35 = (bf16[1536,2048]{1,0:T(8,128)(2,1)S(1)}, bf16[1536,2048]{1,0:T(8,128)(2,1)}, u32[]{:S(2)}) copy-start(bf16[1536,2048]{1,0:T(8,128)(2,1)} %get-tuple-element.63) | copy-start | bytes 18874372
  235.5 153.4 %copy-start.26 = (f32[1024]{0:T(1024)S(1)}, f32[1024]{0:T(1024)}, u32[]{:S(2)}) copy-start(f32[1024]{0:T(1024)} %param.31) | copy-start | bytes 12292
  235.5 307.7 %all-reduce.12.cloned.1.call-start = ((), (), s32[]{:S(2)}) async-start(), calls=%async_computation.1 | async-start | bytes 5767168 | tf_op jit(solution)/shard_map/psum | solution.py:220
  388.9 14.4 %copy-start.3 = (bf16[1,1536,1024]{2,1,0:T(8,128)(2,1)S(1)}, bf16[1,1536,1024]{2,1,0:T(8,128)(2,1)}, u32[]{:S(2)}) copy-start(bf16[1,1536,1024]{2,1,0:T(8,128)(2,1)} %param.17) | copy-start | bytes 9437188
  388.9 14.4 %copy-start.5 = (bf16[1536,1024]{1,0:T(8,128)(2,1)S(1)}, bf16[1536,1024]{1,0:T(8,128)(2,1)}, u32[]{:S(2)}) copy-start(bf16[1536,1024]{1,0:T(8,128)(2,1)} %all-reduce.10.cloned.1.call-done) | copy-start | bytes 9437188
  388.9 14.4 %copy-start.6 = (bf16[1536,1024]{1,0:T(8,128)(2,1)S(1)}, bf16[1536,1024]{1,0:T(8,128)(2,1)}, u32[]{:S(2)}) copy-start(bf16[1536,1024]{1,0:T(8,128)(2,1)} %get-tuple-element.61) | copy-start | bytes 9437188
  388.9 14.4 %copy-start.8 = (bf16[1,1536,1024]{2,1,0:T(8,128)(2,1)S(1)}, bf16[1,1536,1024]{2,1,0:T(8,128)(2,1)}, u32[]{:S(2)}) copy-start(bf16[1,1536,1024]{2,1,0:T(8,128)(2,1)} %param.33) | copy-start | bytes 9437188
  403.4 5.1 copy-start.32
  408.5 3.2 copy-start.7
  463.0 318.8 %all-reduce.14.cloned.1.call-start = ((), (), s32[]{:S(2)}) async-start(), calls=%async_computation.2 | async-start | bytes 25165824 | tf_op jit(solution)/shard_map/psum | solution.py:247
  463.0 12.3 %copy-start.13 = (bf16[1536,512]{1,0:T(8,128)(2,1)S(1)}, bf16[1536,512]{1,0:T(8,128)(2,1)}, u32[]{:S(2)}) copy-start(bf16[1536,512]{1,0:T(8,128)(2,1)} %get-tuple-element.22.o_ref) | copy-start | bytes 4718596
  475.3 5.8 copy-start.12
  475.3 5.8 copy-start.14
  475.3 5.8 copy-start.15
  475.4 5.8 copy-start.30
  487.8 57.8 %copy-start.17 = (f32[1536]{0:T(1024)S(1)}, f32[1536]{0:T(1024)}, u32[]{:S(2)}) copy-start(f32[1536]{0:T(1024)} %copy-done.16) | copy-start | bytes 18436
  487.8 57.8 %copy-start.19 = (f32[1536]{0:T(1024)S(1)}, f32[1536]{0:T(1024)}, u32[]{:S(2)}) copy-start(f32[1536]{0:T(1024)} %copy-done.18) | copy-start | bytes 18436
  487.9 57.8 %copy-start.23 = (f32[1024]{0:T(1024)S(1)}, f32[1024]{0:T(1024)}, u32[]{:S(2)}) copy-start(f32[1024]{0:T(1024)} %param.19) | copy-start | bytes 12292
  781.8 8.4 %copy-start.10 = (bf16[1024,2048]{1,0:T(8,128)(2,1)S(1)}, bf16[1024,2048]{1,0:T(8,128)(2,1)}, u32[]{:S(2)}) copy-start(bf16[1024,2048]{1,0:T(8,128)(2,1)} %get-tuple-element.58) | copy-start | bytes 12582916
  790.2 4.5 copy-start.9
Sparse Core Ops, SparseCore 0:
  60.6 88.5 all-reduce.9
  235.6 153.2 all-reduce.15
  463.1 80.0 all-reduce.11
  548.8 232.9 all-reduce.13
